TPU v7x, 32 devices: a whole 2x2x4 slice. The times are simulated.
32 devices in a mesh: mem: 8 (over y, x, core), lat: 4 (over z).
Axes of the slice: x: 2, y: 2, z: 4, core: 2. Of those that a mesh axis runs over, the one named last changes fastest.
Arguments:
- coarse_weights: bfloat16 [32, 32, 8, 128], P('lat', 'mem'), may hold values from -6 to 6
- perturbations: bfloat16 [32, 8, 128, 512], P('mem', None, 'lat'), may hold values from -6 to 6
- lat_matrix: bfloat16 [128, 32], P('lat'), may hold values from -1 to 1
- lon_matrix: bfloat16 [128, 512], replicated, may hold values from -0.5 to 0.5
- wind_field: float32 [2, 128, 512], P(None, 'lat', 'mem'), may hold values from -0.4 to 0.4
- observed_cell: int32 [4, 8, 128, 64], P(None, None, 'lat', 'mem'), may hold values from 0 to 7
- observed_value: float32 [4, 8, 128, 64], P(None, None, 'lat', 'mem'), may hold values from -6 to 6
- observed_weight: float32 [4, 8, 128, 64], P(None, None, 'lat', 'mem'), may hold values from 0.5 to 4
Outputs:
- gradient: float32 [32, 32, 8, 128], P('lat', 'mem')
- increment: float32 [8, 128, 512], P(None, 'lat', 'mem')
Inputs may be any that keep to these rules, and one draw needn't show every extreme that they name: `observed_cell`: the observed cell is an offset within its block of 8 longitudes.
All inputs are finite; a program needn't handle non-finite values.
Results may differ from a plain program's by a relative error of at most 0.0003.
Values may be sent and summed in bfloat16 or wider, within the bound.
A program may use at most 64 MiB of HBM per device.

v0:
```python
import jax
import jax.numpy as jnp
from jax import lax
from jax.sharding import PartitionSpec as P

STEPS = 4
OBLK = 8
diffusion = 0.2
highest = lax.Precision.HIGHEST


def padded_2(value, sides, width):
    for axis, dim in sides:
        peers, length = (lax.axis_size(axis), value.shape[dim])
        up = [(i, (i + 1) % peers) for i in range(peers - 1)]
        down = [(j, i) for i, j in up]
        last = lax.slice_in_dim(value, length - width, length, axis=dim)
        initial = lax.slice_in_dim(value, 0, width, axis=dim)
        before = lax.ppermute(last, axis, up)
        after = lax.ppermute(initial, axis, down)
        value = jnp.concatenate([before, value, after], axis=dim)
    return value


def stencil_parts(padded):
    center = padded[:, 1:-1, 1:-1]
    north_cell = padded[:, 2:, 1:-1]
    south_cell = padded[:, :-2, 1:-1]
    east_cell = padded[:, 1:-1, 2:]
    west_cell = padded[:, 1:-1, :-2]
    return (center, north_cell, south_cell, east_cell, west_cell)


def advance(padded, wind_out):
    center, north_cell, south_cell, east_cell, west_cell = stencil_parts(padded)
    spread = north_cell + south_cell + east_cell + west_cell - 4.0 * center
    return (
        center
        + diffusion * spread
        - 0.5 * wind_out[1] * (north_cell - south_cell)
        - 0.5 * wind_out[0] * (east_cell - west_cell)
    )


def retreat(padded, wind_in):
    center, north_cell, south_cell, east_cell, west_cell = stencil_parts(padded)
    spread = north_cell + south_cell + east_cell + west_cell - 4.0 * center
    along_lon = wind_in[0] * padded
    along_lat = wind_in[1] * padded
    return (
        center
        + diffusion * spread
        + 0.5 * (along_lat[:, 2:, 1:-1] - along_lat[:, :-2, 1:-1])
        + 0.5 * (along_lon[:, 1:-1, 2:] - along_lon[:, 1:-1, :-2])
    )


def observe(tangent, picked, observed, weighting):
    levels, row_count, col_count = tangent.shape
    blocks = tangent.reshape(levels, row_count, col_count // OBLK, OBLK)
    onehot = (picked[..., None] == jnp.arange(OBLK, dtype=jnp.int32)).astype(jnp.float32)
    looked = jnp.sum(blocks * onehot, axis=-1)
    misfit = weighting * (looked - observed)
    return (misfit[..., None] * onehot).reshape(levels, row_count, col_count)


def domain_mask(margin, row_count, col_count):
    lat_start = lax.axis_index("lat") * row_count - margin
    lon_start = lax.axis_index("mem") * col_count - margin
    row_place = lat_start + jnp.arange(row_count + 2 * margin, dtype=jnp.int32)
    col_place = lon_start + jnp.arange(col_count + 2 * margin, dtype=jnp.int32)
    rows_inside = (row_place >= 0) & (row_place < row_count * lax.axis_size("lat"))
    cols_inside = (col_place >= 0) & (col_place < col_count * lax.axis_size("mem"))
    return (rows_inside[:, None] & cols_inside[None, :]).astype(jnp.float32)


def body(
    coarse_weights,
    perturbations,
    lat_matrix,
    lon_matrix,
    wind_field,
    observed_cell,
    observed_value,
    observed_weight,
):
    members_here, levels, row_count, lon_total = perturbations.shape
    col_count = wind_field.shape[2]
    members_all = members_here * lax.axis_size("mem")
    member_scale = 1.0 / jnp.sqrt(jnp.float32(members_all - 1))
    lat_full = lat_matrix.astype(jnp.float32)
    lon_full = lon_matrix.astype(jnp.float32)
    widened = jnp.einsum(
        "cmlw,wf->cmlf", coarse_weights.astype(jnp.float32), lon_full, precision=highest
    )
    columns = lat_full
    localized = jnp.einsum(
        "rc,cmlf->mlrf",
        columns,
        lax.all_gather(widened, "lat", axis=0, tiled=True),
        precision=highest,
    )
    partial_sum = jnp.sum(localized * perturbations, axis=0)
    increment = lax.psum_scatter(partial_sum, "mem", scatter_dimension=2, tiled=True) * member_scale
    wide_wind = padded_2(wind_field, (("mem", 2), ("lat", 1)), STEPS)

    def wind_margin(margin):
        return wide_wind[
            :,
            STEPS - margin : STEPS + row_count + margin,
            STEPS - margin : STEPS + col_count + margin,
        ]

    forcings = []
    tangent = padded_2(increment, (("mem", 2), ("lat", 1)), STEPS)
    for step_index in range(STEPS):
        margin = STEPS - step_index - 1
        tangent = advance(tangent, wind_margin(margin)) * domain_mask(margin, row_count, col_count)
        inner = tangent[:, margin : margin + row_count, margin : margin + col_count]
        forcings.append(
            observe(
                inner,
                observed_cell[step_index],
                observed_value[step_index],
                observed_weight[step_index],
            )
        )
    adjoint = jnp.zeros_like(increment)
    for step_index in reversed(range(STEPS)):
        padded = padded_2(adjoint + forcings[step_index], (("mem", 2), ("lat", 1)), 1)
        adjoint = retreat(padded, wind_margin(1))
    product = perturbations * lax.all_gather(adjoint, "mem", axis=2, tiled=True)[None]
    projected = jnp.einsum("mlrf,wf->mlrw", product, lon_full, precision=highest)
    columns = lat_full
    banded = lax.psum_scatter(
        jnp.einsum("rc,mlrw->cmlw", columns, projected, precision=highest),
        "lat",
        scatter_dimension=0,
        tiled=True,
    )
    gradient = banded * member_scale + coarse_weights.astype(jnp.float32)
    return (gradient, increment)


def solution(mesh):
    in_specs = (
        P("lat", "mem", None, None),
        P("mem", None, "lat", None),
        P("lat", None),
        P(),
        P(None, "lat", "mem"),
        P(None, None, "lat", "mem"),
        P(None, None, "lat", "mem"),
        P(None, None, "lat", "mem"),
    )
    out_specs = (P("lat", "mem", None, None), P(None, "lat", "mem"))
    return jax.shard_map(body, mesh=mesh, in_specs=in_specs, out_specs=out_specs, check_vma=False)
```

profile of v0, /device:TPU:0, one launch (start us, length us, event | category | flops | bytes accessed | tf_op | source)
XLA Modules:
  0.0 257.9 jit_solution(16076721269377844049)
XLA Ops:
  8.1 1.9 fusion.53
  10.0 1.5 fusion.76
  11.5 2.4 collective-permute-start.4
  13.9 1.3 collective-permute-start.5
  19.0 39.5 %all-gather.2.cloned.1.call-done = f32[32,4,8,512]{3,0,2,1:T(8,128)} async-done(((f32[8,4,8,512]{3,0,2,1:T(8,128)}), f32[32,4,8,512]{3,0,2,1:T(8,128)}) %all-gather.2.cloned.1.call-update) | async-done | bytes 2097168 | tf_op jit(solution)/shard_map/all_gather | solution.py:100
  58.5 3.7 %fusion = f32[8,32,512]{2,1,0:T(8,128)} fusion(bf16[4,8,32,512]{3,2,1,0:T(8,128)(2,1)S(1)} %copy-done.1, f32[32,4,8,512]{3,0,2,1:T(8,128)} %all-gather.2.cloned.1.call-done, bf16[32,32]{1,0:T(8,128)(2,1)} %param.10), kind=kOutput, calls=%fused_computation.2 | convolution fusion | flops 202768384 | bytes 3672064 | tf_op jit(solution)/shard_map/rc,cmlf->mlrf/dot_general | solution.py:97
  62.2 1.8 copy.254
  64.1 1.4 reshape.260
  65.7 2.1 collective-permute-start.6
  67.8 1.3 collective-permute-start.7
  69.4 3.9 %collective-permute-done.7 = f32[2,4,72]{2,1,0:T(4,128)S(1)} collective-permute-done((f32[2,4,72]{2,1,0:T(4,128)S(1)}, f32[2,4,72]{2,1,0:T(4,128)S(1)}, u32[]{:S(2)}, u32[]{:S(2)}) %collective-permute-start.7) | collective-permute-done | bytes 2336 | tf_op jit(solution)/shard_map/ppermute | solution.py:20
  74.2 24.3 %reduce-scatter.7.cloned.1.call-done = f32[64,256]{1,0:T(8,128)} async-done(((f32[512,256]{1,0:T(8,128)}), f32[64,256]{1,0:T(8,128)}) %reduce-scatter.7.cloned.1.call-update) | async-done | bytes 65552
  99.8 1.3 collective-permute-start
  101.1 1.3 collective-permute-start.1
  102.5 3.5 %collective-permute-done.1 = f32[8,32,4]{2,1,0:T(8,128)S(1)} collective-permute-done((f32[8,32,4]{2,1,0:T(8,128)S(1)}, f32[8,32,4]{2,1,0:T(8,128)S(1)}, u32[]{:S(2)}, u32[]{:S(2)}) %collective-permute-start.1) | collective-permute-done | bytes 4128 | tf_op jit(solution)/shard_map/ppermute | solution.py:20
  106.3 3.4 %collective-permute-start.2 = (f32[8,4,72]{1,2,0:T(8,128)S(1)}, f32[8,4,72]{1,2,0:T(8,128)S(1)}, u32[]{:S(2)}, u32[]{:S(2)}) collective-permute-start(f32[8,4,72]{1,2,0:T(8,128)S(1)} %copy.233), channel_id=1, source_target_pairs={{0,1},{1,2},{2,3},{4,5},{5,6},{6,7},{8,9},{9,10},{10,11},{12,13},{... | collective-permute-start | bytes 27656 | tf_op jit(solution)/shard_map/ppermute | solution.py:19
  109.9 1.3 collective-permute-start.3
  112.1 2.5 collective-permute-done.2
  114.6 4.9 %collective-permute-done.3 = f32[8,4,72]{1,2,0:T(8,128)S(1)} collective-permute-done((f32[8,4,72]{1,2,0:T(8,128)S(1)}, f32[8,4,72]{1,2,0:T(8,128)S(1)}, u32[]{:S(2)}, u32[]{:S(2)}) %collective-permute-start.3) | collective-permute-done | bytes 9248 | tf_op jit(solution)/shard_map/ppermute | solution.py:20
  121.7 4.0 %collective-permute-start.8 = (f32[8,32,1]{1,2,0:T(1,128)S(1)}, f32[8,32,1]{1,2,0:T(1,128)S(1)}, u32[]{:S(2)}, u32[]{:S(2)}) collective-permute-start(f32[8,32,1]{1,2,0:T(1,128)S(1)} %get-tuple-element.40), channel_id=1, source_target_pairs={{0,4},{4,8},{8,12},{12,16},{16,20},{20,24},{24,28},{1,5},{5,9},{9,... | collective-permute-start | bytes 3080 | tf_op jit(solution)/shard_map/ppermute | solution.py:19
  125.8 1.3 collective-permute-start.9
  127.1 3.5 %collective-permute-done.9 = f32[8,32,1]{1,2,0:T(1,128)S(1)} collective-permute-done((f32[8,32,1]{1,2,0:T(1,128)S(1)}, f32[8,32,1]{1,2,0:T(1,128)S(1)}, u32[]{:S(2)}, u32[]{:S(2)}) %collective-permute-start.9) | collective-permute-done | bytes 1056 | tf_op jit(solution)/shard_map/ppermute | solution.py:20
  130.8 1.3 collective-permute-start.10
  132.1 4.6 %collective-permute-start.11 = (f32[8,1,66]{1,2,0:T(8,128)S(1)}, f32[8,1,66]{1,2,0:T(8,128)S(1)}, u32[]{:S(2)}, u32[]{:S(2)}) collective-permute-start(f32[8,1,66]{1,2,0:T(8,128)S(1)} %get-tuple-element.28), channel_id=1, source_target_pairs={{0,1},{1,2},{2,3},{4,5},{5,6},{6,7},{8,9},{9,10},{10,11},{12,13},{... | collective-permute-start | bytes 6344 | tf_op jit(solution)/shard_map/ppermute | solution.py:19
  136.8 4.3 %collective-permute-done.10 = f32[8,1,66]{1,2,0:T(8,128)S(1)} collective-permute-done((f32[8,1,66]{1,2,0:T(8,128)S(1)}, f32[8,1,66]{1,2,0:T(8,128)S(1)}, u32[]{:S(2)}, u32[]{:S(2)}) %collective-permute-start.10) | collective-permute-done | bytes 2144 | tf_op jit(solution)/shard_map/ppermute | solution.py:20
  141.1 1.7 collective-permute-done.11
  143.7 3.1 %collective-permute-start.12 = (f32[8,32,1]{1,2,0:T(1,128)S(1)}, f32[8,32,1]{1,2,0:T(1,128)S(1)}, u32[]{:S(2)}, u32[]{:S(2)}) collective-permute-start(f32[8,32,1]{1,2,0:T(1,128)S(1)} %get-tuple-element.38), channel_id=1, source_target_pairs={{0,4},{4,8},{8,12},{12,16},{16,20},{20,24},{24,28},{1,5},{5,9},{9,... | collective-permute-start | bytes 3080 | tf_op jit(solution)/shard_map/ppermute | solution.py:19
  148.1 1.8 collective-permute-done.13
  150.1 1.3 collective-permute-start.14
  151.4 4.9 %collective-permute-start.15 = (f32[8,1,66]{1,2,0:T(8,128)S(1)}, f32[8,1,66]{1,2,0:T(8,128)S(1)}, u32[]{:S(2)}, u32[]{:S(2)}) collective-permute-start(f32[8,1,66]{1,2,0:T(8,128)S(1)} %get-tuple-element.26), channel_id=1, source_target_pairs={{0,1},{1,2},{2,3},{4,5},{5,6},{6,7},{8,9},{9,10},{10,11},{12,13},{... | collective-permute-start | bytes 6344 | tf_op jit(solution)/shard_map/ppermute | solution.py:19
  156.3 4.1 %collective-permute-done.14 = f32[8,1,66]{1,2,0:T(8,128)S(1)} collective-permute-done((f32[8,1,66]{1,2,0:T(8,128)S(1)}, f32[8,1,66]{1,2,0:T(8,128)S(1)}, u32[]{:S(2)}, u32[]{:S(2)}) %collective-permute-start.14) | collective-permute-done | bytes 2144 | tf_op jit(solution)/shard_map/ppermute | solution.py:20
  160.4 1.7 collective-permute-done.15
  162.9 3.5 %collective-permute-start.16 = (f32[8,32,1]{1,2,0:T(1,128)S(1)}, f32[8,32,1]{1,2,0:T(1,128)S(1)}, u32[]{:S(2)}, u32[]{:S(2)}) collective-permute-start(f32[8,32,1]{1,2,0:T(1,128)S(1)} %get-tuple-element.36), channel_id=1, source_target_pairs={{0,4},{4,8},{8,12},{12,16},{16,20},{20,24},{24,28},{1,5},{5,9},{9,... | collective-permute-start | bytes 3080 | tf_op jit(solution)/shard_map/ppermute | solution.py:19
  167.8 1.8 collective-permute-done.17
  169.7 1.3 collective-permute-start.18
  171.0 5.0 %collective-permute-start.19 = (f32[8,1,66]{1,2,0:T(8,128)S(1)}, f32[8,1,66]{1,2,0:T(8,128)S(1)}, u32[]{:S(2)}, u32[]{:S(2)}) collective-permute-start(f32[8,1,66]{1,2,0:T(8,128)S(1)} %get-tuple-element.24), channel_id=1, source_target_pairs={{0,1},{1,2},{2,3},{4,5},{5,6},{6,7},{8,9},{9,10},{10,11},{12,13},{... | collective-permute-start | bytes 6344 | tf_op jit(solution)/shard_map/ppermute | solution.py:19
  176.0 4.2 %collective-permute-done.18 = f32[8,1,66]{1,2,0:T(8,128)S(1)} collective-permute-done((f32[8,1,66]{1,2,0:T(8,128)S(1)}, f32[8,1,66]{1,2,0:T(8,128)S(1)}, u32[]{:S(2)}, u32[]{:S(2)}) %collective-permute-start.18) | collective-permute-done | bytes 2144 | tf_op jit(solution)/shard_map/ppermute | solution.py:20
  180.2 1.7 collective-permute-done.19
  182.7 3.5 %collective-permute-start.20 = (f32[8,32,1]{1,2,0:T(1,128)S(1)}, f32[8,32,1]{1,2,0:T(1,128)S(1)}, u32[]{:S(2)}, u32[]{:S(2)}) collective-permute-start(f32[8,32,1]{1,2,0:T(1,128)S(1)} %get-tuple-element.30), channel_id=1, source_target_pairs={{0,4},{4,8},{8,12},{12,16},{16,20},{20,24},{24,28},{1,5},{5,9},{9,... | collective-permute-start | bytes 3080 | tf_op jit(solution)/shard_map/ppermute | solution.py:19
  186.2 1.3 collective-permute-start.21
  187.5 2.0 collective-permute-done.21
  190.9 5.0 %collective-permute-start.23 = (f32[8,1,66]{1,2,0:T(8,128)S(1)}, f32[8,1,66]{1,2,0:T(8,128)S(1)}, u32[]{:S(2)}, u32[]{:S(2)}) collective-permute-start(f32[8,1,66]{1,2,0:T(8,128)S(1)} %get-tuple-element.22), channel_id=1, source_target_pairs={{0,1},{1,2},{2,3},{4,5},{5,6},{6,7},{8,9},{9,10},{10,11},{12,13},{... | collective-permute-start | bytes 6344 | tf_op jit(solution)/shard_map/ppermute | solution.py:19
  196.0 4.2 %collective-permute-done.22 = f32[8,1,66]{1,2,0:T(8,128)S(1)} collective-permute-done((f32[8,1,66]{1,2,0:T(8,128)S(1)}, f32[8,1,66]{1,2,0:T(8,128)S(1)}, u32[]{:S(2)}, u32[]{:S(2)}) %collective-permute-start.22) | collective-permute-done | bytes 2144 | tf_op jit(solution)/shard_map/ppermute | solution.py:20
  200.2 1.7 collective-permute-done.23
  202.7 17.4 %all_gather.7 = f32[8,32,512]{1,2,0:T(8,128)S(1)} all-gather(f32[8,32,64]{1,2,0:T(8,128)S(1)} %fusion.4), channel_id=1, replica_groups=mesh['mem'=8,'lat'=4] {'mem'}, dimensions={2}, use_global_device_ids=true | all-gather | bytes 589824 | tf_op jit(solution)/shard_map/all_gather | solution.py:132
  220.1 1.4 copy.246
  221.5 2.2 fusion.1
  225.0 24.8 %reduce-scatter.5.cloned.1.call-done = f32[8,4,8,128]{3,0,2,1:T(8,128)} async-done(((f32[32,4,8,128]{3,0,2,1:T(8,128)}), f32[8,4,8,128]{3,0,2,1:T(8,128)}) %reduce-scatter.5.cloned.1.call-update) | async-done | bytes 131088 | tf_op jit(solution)/shard_map/reduce_scatter | solution.py:135
  (114 shorter events, 21.6 us)
Async XLA Ops:
  7.2 0.9 copy-start
  7.2 51.3 %copy-start.1 = (bf16[4,8,32,512]{3,2,1,0:T(8,128)(2,1)S(1)}, bf16[4,8,32,512]{3,2,1,0:T(8,128)(2,1)}, u32[]{:S(2)}) copy-start(bf16[4,8,32,512]{3,2,1,0:T(8,128)(2,1)} %param.9) | copy-start | bytes 3145732
  7.2 51.3 %all-gather.2.cloned.1.call-start = ((), (), s32[]{:S(2)}) async-start(), calls=%async_computation.2 | async-start | bytes 2621440 | tf_op jit(solution)/shard_map/all_gather | solution.py:100
  10.0 88.6 %reduce-scatter.7.cloned.1.call-start = ((), (), s32[]{:S(2)}) async-start(), calls=%async_computation.4 | async-start | bytes 589824
  11.5 54.0 %collective-permute-start.4 = (f32[2,32,4]{2,1,0:T(8,128)}, f32[2,32,4]{2,1,0:T(8,128)S(1)}, u32[]{:S(2)}, u32[]{:S(2)}) collective-permute-start(f32[2,32,4]{2,1,0:T(8,128)} %get-tuple-element.62), channel_id=1, source_target_pairs={{0,4},{4,8},{8,12},{12,16},{16,20},{20,24},{24,28},{1,5},{5,9},{9,... | collective-permute-start | bytes 3080 | tf_op jit(solution)/shard_map/ppermute | solution.py:19
  13.9 51.6 %collective-permute-start.5 = (f32[2,32,4]{2,1,0:T(8,128)}, f32[2,32,4]{2,1,0:T(8,128)S(1)}, u32[]{:S(2)}, u32[]{:S(2)}) collective-permute-start(f32[2,32,4]{2,1,0:T(8,128)} %get-tuple-element.63), channel_id=1, source_target_pairs={{4,0},{8,4},{12,8},{16,12},{20,16},{24,20},{28,24},{5,1},{9,5},{13... | collective-permute-start | bytes 3080 | tf_op jit(solution)/shard_map/ppermute | solution.py:20
  64.1 1.5 copy-start.3
  65.5 184.3 %reduce-scatter.5.cloned.1.call-start = ((), (), s32[]{:S(2)}) async-start(), calls=%async_computation.3 | async-start | bytes 655360 | tf_op jit(solution)/shard_map/reduce_scatter | solution.py:135
  65.6 2.2 copy-start.8
  65.6 3.6 %copy-start.9 = (f32[2,32,4]{2,1,0:T(8,128)}, f32[2,32,4]{2,1,0:T(8,128)S(1)}, u32[]{:S(2)}) copy-start(f32[2,32,4]{2,1,0:T(8,128)S(1)} %collective-permute-done.5) | copy-start | bytes 3076
  65.7 3.7 %collective-permute-start.6 = (f32[2,4,72]{2,1,0:T(4,128)S(1)}, f32[2,4,72]{2,1,0:T(4,128)S(1)}, u32[]{:S(2)}, u32[]{:S(2)}) collective-permute-start(f32[2,4,72]{2,1,0:T(4,128)S(1)} %get-tuple-element.50), channel_id=1, source_target_pairs={{0,1},{1,2},{2,3},{4,5},{5,6},{6,7},{8,9},{9,10},{10,11},{12,13},{... | collective-permute-start | bytes 6920 | tf_op jit(solution)/shard_map/ppermute | solution.py:19
  67.8 5.5 %collective-permute-start.7 = (f32[2,4,72]{2,1,0:T(4,128)S(1)}, f32[2,4,72]{2,1,0:T(4,128)S(1)}, u32[]{:S(2)}, u32[]{:S(2)}) collective-permute-start(f32[2,4,72]{2,1,0:T(4,128)S(1)} %get-tuple-element.51), channel_id=1, source_target_pairs={{1,0},{2,1},{3,2},{5,4},{6,5},{7,6},{9,8},{10,9},{11,10},{13,12},{... | collective-permute-start | bytes 6920 | tf_op jit(solution)/shard_map/ppermute | solution.py:20
  99.6 20.0 %copy-start.7 = (f32[38,70]{0,1:T(8,128)S(1)}, f32[38,70]{0,1:T(8,128)}, u32[]{:S(2)}) copy-start(f32[38,70]{0,1:T(8,128)} %and_convert_fusion.2) | copy-start | bytes 31924
  99.7 20.4 %copy-start.2 = (f32[8,32,64]{2,1,0:T(8,128)}, f32[8,32,64]{2,1,0:T(8,128)S(1)}, u32[]{:S(2)}) copy-start(f32[8,32,64]{2,1,0:T(8,128)S(1)} %broadcast_multiply_fusion.8) | copy-start | bytes 196612
  99.8 2.7 %collective-permute-start = (f32[8,32,4]{2,1,0:T(8,128)S(1)}, f32[8,32,4]{2,1,0:T(8,128)S(1)}, u32[]{:S(2)}, u32[]{:S(2)}) collective-permute-start(f32[8,32,4]{2,1,0:T(8,128)S(1)} %get-tuple-element.48), channel_id=1, source_target_pairs={{0,4},{4,8},{8,12},{12,16},{16,20},{20,24},{24,28},{1,5},{5,9},{9,... | collective-permute-start | bytes 12296 | tf_op jit(solution)/shard_map/ppermute | solution.py:19
  101.1 4.9 %collective-permute-start.1 = (f32[8,32,4]{2,1,0:T(8,128)S(1)}, f32[8,32,4]{2,1,0:T(8,128)S(1)}, u32[]{:S(2)}, u32[]{:S(2)}) collective-permute-start(f32[8,32,4]{2,1,0:T(8,128)S(1)} %get-tuple-element.49), channel_id=1, source_target_pairs={{4,0},{8,4},{12,8},{16,12},{20,16},{24,20},{28,24},{5,1},{9,5},{13... | collective-permute-start | bytes 12296 | tf_op jit(solution)/shard_map/ppermute | solution.py:20
  106.3 8.2 %collective-permute-start.2 = (f32[8,4,72]{1,2,0:T(8,128)S(1)}, f32[8,4,72]{1,2,0:T(8,128)S(1)}, u32[]{:S(2)}, u32[]{:S(2)}) collective-permute-start(f32[8,4,72]{1,2,0:T(8,128)S(1)} %copy.233), channel_id=1, source_target_pairs={{0,1},{1,2},{2,3},{4,5},{5,6},{6,7},{8,9},{9,10},{10,11},{12,13},{... | collective-permute-start | bytes 27656 | tf_op jit(solution)/shard_map/ppermute | solution.py:19
  109.8 10.3 %copy-start.6 = (f32[36,68]{0,1:T(8,128)S(1)}, f32[36,68]{0,1:T(8,128)}, u32[]{:S(2)}) copy-start(f32[36,68]{0,1:T(8,128)} %and_convert_fusion.1) | copy-start | bytes 29380
  109.9 9.5 %collective-permute-start.3 = (f32[8,4,72]{1,2,0:T(8,128)S(1)}, f32[8,4,72]{1,2,0:T(8,128)S(1)}, u32[]{:S(2)}, u32[]{:S(2)}) collective-permute-start(f32[8,4,72]{1,2,0:T(8,128)S(1)} %copy.234), channel_id=1, source_target_pairs={{1,0},{2,1},{3,2},{5,4},{6,5},{7,6},{9,8},{10,9},{11,10},{13,12},{... | collective-permute-start | bytes 27656 | tf_op jit(solution)/shard_map/ppermute | solution.py:20
  119.7 1.1 copy-start.5
  120.5 1.1 copy-start.10
  120.5 1.1 copy-start.11
  121.7 5.3 %collective-permute-start.8 = (f32[8,32,1]{1,2,0:T(1,128)S(1)}, f32[8,32,1]{1,2,0:T(1,128)S(1)}, u32[]{:S(2)}, u32[]{:S(2)}) collective-permute-start(f32[8,32,1]{1,2,0:T(1,128)S(1)} %get-tuple-element.40), channel_id=1, source_target_pairs={{0,4},{4,8},{8,12},{12,16},{16,20},{20,24},{24,28},{1,5},{5,9},{9,... | collective-permute-start | bytes 3080 | tf_op jit(solution)/shard_map/ppermute | solution.py:19
  125.8 4.8 %collective-permute-start.9 = (f32[8,32,1]{1,2,0:T(1,128)S(1)}, f32[8,32,1]{1,2,0:T(1,128)S(1)}, u32[]{:S(2)}, u32[]{:S(2)}) collective-permute-start(f32[8,32,1]{1,2,0:T(1,128)S(1)} %get-tuple-element.41), channel_id=1, source_target_pairs={{4,0},{8,4},{12,8},{16,12},{20,16},{24,20},{28,24},{5,1},{9,5},{13... | collective-permute-start | bytes 3080 | tf_op jit(solution)/shard_map/ppermute | solution.py:20
  130.8 10.4 %collective-permute-start.10 = (f32[8,1,66]{1,2,0:T(8,128)S(1)}, f32[8,1,66]{1,2,0:T(8,128)S(1)}, u32[]{:S(2)}, u32[]{:S(2)}) collective-permute-start(f32[8,1,66]{1,2,0:T(8,128)S(1)} %get-tuple-element.29), channel_id=1, source_target_pairs={{1,0},{2,1},{3,2},{5,4},{6,5},{7,6},{9,8},{10,9},{11,10},{13,12},{... | collective-permute-start | bytes 6344 | tf_op jit(solution)/shard_map/ppermute | solution.py:20
  132.1 10.8 %collective-permute-start.11 = (f32[8,1,66]{1,2,0:T(8,128)S(1)}, f32[8,1,66]{1,2,0:T(8,128)S(1)}, u32[]{:S(2)}, u32[]{:S(2)}) collective-permute-start(f32[8,1,66]{1,2,0:T(8,128)S(1)} %get-tuple-element.28), channel_id=1, source_target_pairs={{0,1},{1,2},{2,3},{4,5},{5,6},{6,7},{8,9},{9,10},{10,11},{12,13},{... | collective-permute-start | bytes 6344 | tf_op jit(solution)/shard_map/ppermute | solution.py:19
  143.7 4.5 %collective-permute-start.12 = (f32[8,32,1]{1,2,0:T(1,128)S(1)}, f32[8,32,1]{1,2,0:T(1,128)S(1)}, u32[]{:S(2)}, u32[]{:S(2)}) collective-permute-start(f32[8,32,1]{1,2,0:T(1,128)S(1)} %get-tuple-element.38), channel_id=1, source_target_pairs={{0,4},{4,8},{8,12},{12,16},{16,20},{20,24},{24,28},{1,5},{5,9},{9,... | collective-permute-start | bytes 3080 | tf_op jit(solution)/shard_map/ppermute | solution.py:19
  146.8 3.1 %collective-permute-start.13 = (f32[8,32,1]{1,2,0:T(1,128)S(1)}, f32[8,32,1]{1,2,0:T(1,128)S(1)}, u32[]{:S(2)}, u32[]{:S(2)}) collective-permute-start(f32[8,32,1]{1,2,0:T(1,128)S(1)} %get-tuple-element.39), channel_id=1, source_target_pairs={{4,0},{8,4},{12,8},{16,12},{20,16},{24,20},{28,24},{5,1},{9,5},{13... | collective-permute-start | bytes 3080 | tf_op jit(solution)/shard_map/ppermute | solution.py:20
  150.1 10.3 %collective-permute-start.14 = (f32[8,1,66]{1,2,0:T(8,128)S(1)}, f32[8,1,66]{1,2,0:T(8,128)S(1)}, u32[]{:S(2)}, u32[]{:S(2)}) collective-permute-start(f32[8,1,66]{1,2,0:T(8,128)S(1)} %get-tuple-element.27), channel_id=1, source_target_pairs={{1,0},{2,1},{3,2},{5,4},{6,5},{7,6},{9,8},{10,9},{11,10},{13,12},{... | collective-permute-start | bytes 6344 | tf_op jit(solution)/shard_map/ppermute | solution.py:20
  151.4 10.8 %collective-permute-start.15 = (f32[8,1,66]{1,2,0:T(8,128)S(1)}, f32[8,1,66]{1,2,0:T(8,128)S(1)}, u32[]{:S(2)}, u32[]{:S(2)}) collective-permute-start(f32[8,1,66]{1,2,0:T(8,128)S(1)} %get-tuple-element.26), channel_id=1, source_target_pairs={{0,1},{1,2},{2,3},{4,5},{5,6},{6,7},{8,9},{9,10},{10,11},{12,13},{... | collective-permute-start | bytes 6344 | tf_op jit(solution)/shard_map/ppermute | solution.py:19
  162.9 4.8 %collective-permute-start.16 = (f32[8,32,1]{1,2,0:T(1,128)S(1)}, f32[8,32,1]{1,2,0:T(1,128)S(1)}, u32[]{:S(2)}, u32[]{:S(2)}) collective-permute-start(f32[8,32,1]{1,2,0:T(1,128)S(1)} %get-tuple-element.36), channel_id=1, source_target_pairs={{0,4},{4,8},{8,12},{12,16},{16,20},{20,24},{24,28},{1,5},{5,9},{9,... | collective-permute-start | bytes 3080 | tf_op jit(solution)/shard_map/ppermute | solution.py:19
  166.5 3.1 %collective-permute-start.17 = (f32[8,32,1]{1,2,0:T(1,128)S(1)}, f32[8,32,1]{1,2,0:T(1,128)S(1)}, u32[]{:S(2)}, u32[]{:S(2)}) collective-permute-start(f32[8,32,1]{1,2,0:T(1,128)S(1)} %get-tuple-element.37), channel_id=1, source_target_pairs={{4,0},{8,4},{12,8},{16,12},{20,16},{24,20},{28,24},{5,1},{9,5},{13... | collective-permute-start | bytes 3080 | tf_op jit(solution)/shard_map/ppermute | solution.py:20
  169.7 10.4 %collective-permute-start.18 = (f32[8,1,66]{1,2,0:T(8,128)S(1)}, f32[8,1,66]{1,2,0:T(8,128)S(1)}, u32[]{:S(2)}, u32[]{:S(2)}) collective-permute-start(f32[8,1,66]{1,2,0:T(8,128)S(1)} %get-tuple-element.25), channel_id=1, source_target_pairs={{1,0},{2,1},{3,2},{5,4},{6,5},{7,6},{9,8},{10,9},{11,10},{13,12},{... | collective-permute-start | bytes 6344 | tf_op jit(solution)/shard_map/ppermute | solution.py:20
  171.0 10.9 %collective-permute-start.19 = (f32[8,1,66]{1,2,0:T(8,128)S(1)}, f32[8,1,66]{1,2,0:T(8,128)S(1)}, u32[]{:S(2)}, u32[]{:S(2)}) collective-permute-start(f32[8,1,66]{1,2,0:T(8,128)S(1)} %get-tuple-element.24), channel_id=1, source_target_pairs={{0,1},{1,2},{2,3},{4,5},{5,6},{6,7},{8,9},{9,10},{10,11},{12,13},{... | collective-permute-start | bytes 6344 | tf_op jit(solution)/shard_map/ppermute | solution.py:19
  182.7 4.8 %collective-permute-start.20 = (f32[8,32,1]{1,2,0:T(1,128)S(1)}, f32[8,32,1]{1,2,0:T(1,128)S(1)}, u32[]{:S(2)}, u32[]{:S(2)}) collective-permute-start(f32[8,32,1]{1,2,0:T(1,128)S(1)} %get-tuple-element.30), channel_id=1, source_target_pairs={{0,4},{4,8},{8,12},{12,16},{16,20},{20,24},{24,28},{1,5},{5,9},{9,... | collective-permute-start | bytes 3080 | tf_op jit(solution)/shard_map/ppermute | solution.py:19
  186.2 3.3 %collective-permute-start.21 = (f32[8,32,1]{1,2,0:T(1,128)S(1)}, f32[8,32,1]{1,2,0:T(1,128)S(1)}, u32[]{:S(2)}, u32[]{:S(2)}) collective-permute-start(f32[8,32,1]{1,2,0:T(1,128)S(1)} %get-tuple-element.31), channel_id=1, source_target_pairs={{4,0},{8,4},{12,8},{16,12},{20,16},{24,20},{28,24},{5,1},{9,5},{13... | collective-permute-start | bytes 3080 | tf_op jit(solution)/shard_map/ppermute | solution.py:20
  189.6 10.6 %collective-permute-start.22 = (f32[8,1,66]{1,2,0:T(8,128)S(1)}, f32[8,1,66]{1,2,0:T(8,128)S(1)}, u32[]{:S(2)}, u32[]{:S(2)}) collective-permute-start(f32[8,1,66]{1,2,0:T(8,128)S(1)} %get-tuple-element.23), channel_id=1, source_target_pairs={{1,0},{2,1},{3,2},{5,4},{6,5},{7,6},{9,8},{10,9},{11,10},{13,12},{... | collective-permute-start | bytes 6344 | tf_op jit(solution)/shard_map/ppermute | solution.py:20
  190.9 11.0 %collective-permute-start.23 = (f32[8,1,66]{1,2,0:T(8,128)S(1)}, f32[8,1,66]{1,2,0:T(8,128)S(1)}, u32[]{:S(2)}, u32[]{:S(2)}) collective-permute-start(f32[8,1,66]{1,2,0:T(8,128)S(1)} %get-tuple-element.22), channel_id=1, source_target_pairs={{0,1},{1,2},{2,3},{4,5},{5,6},{6,7},{8,9},{9,10},{10,11},{12,13},{... | collective-permute-start | bytes 6344 | tf_op jit(solution)/shard_map/ppermute | solution.py:19
  220.1 3.6 %copy-start.12 = (bf16[32,32]{1,0:T(8,128)(2,1)S(1)}, bf16[32,32]{1,0:T(8,128)(2,1)}, u32[]{:S(2)}) copy-start(bf16[32,32]{1,0:T(8,128)(2,1)} %param.10) | copy-start | bytes 6148
  221.5 28.3 %copy-start.4 = (bf16[8,4,8,128]{3,2,1,0:T(8,128)(2,1)S(1)}, bf16[8,4,8,128]{3,2,1,0:T(8,128)(2,1)}, u32[]{:S(2)}) copy-start(bf16[8,4,8,128]{3,2,1,0:T(8,128)(2,1)} %param.8) | copy-start | bytes 196612
Sparse Core Ops, SparseCore 0:
  10.1 48.3 all-gather.1
  65.6 32.8 reduce-scatter.6
  225.1 24.6 reduce-scatter.4
where the time goes:
time: 259 us; the launch traced here: 258 us
  waiting for transfers between devices  136 us (53%)
  starting transfers between devices  58.4 us (23%)
  blocking collectives  17.4 us (7%)
  between operations  14.5 us (6%)
  local copies, waits for them, and re-layouts  11.8 us (5%)
  other arithmetic  10.6 us (4%)
  matrix products  9.04 us (3%)
    ppermute x12, starting transfers between devices, padded_2(): before = lax.ppermute(last, axis, up)  42.8 us
    all_gather x1, waiting for transfers between devices, body(): lax.all_gather(widened, 'lat', axis=0, tiled=True)  39.5 us
    ppermute x12, waiting for transfers between devices, padded_2(): after = lax.ppermute(initial, axis, down)  38.1 us
    reduce_scatter x1, waiting for transfers between devices, body(): lax.psum_scatter(jnp.einsum('rc,mlrw->cmlw', columns, projected, precisio...  24.8 us
    unnamed x4, waiting for transfers between devices  24.4 us
    all_gather x1, blocking collectives, body(): lax.all_gather(adjoint, 'mem', axis=2, tiled=True)[None]  17.4 us
    ppermute x12, starting transfers between devices, padded_2(): after = lax.ppermute(initial, axis, down)  15.5 us
    ppermute x12, waiting for transfers between devices, padded_2(): before = lax.ppermute(last, axis, up)  9.46 us
  transfers between devices with their start and end apart: 27, of which 19 were waited for; matrix products, arithmetic and copies ran while one was open for 6% of the time, Pallas kernels for 0%

commit v1 on v0

--- a/solution.py
+++ b/solution.py
@@ -7,6 +7,27 @@
 OBLK = 8
 diffusion = 0.2
 highest = lax.Precision.HIGHEST
+
+
+def gather_around(x, axis, dim):
+    size, position, rows = (lax.axis_size(axis), lax.axis_index(axis), x.shape[dim])
+    right = [(i, (i + 1) % size) for i in range(size)]
+    behind = [(i, (i - 1) % size) for i in range(size)]
+    out = jnp.zeros((*x.shape[:dim], size * rows, *x.shape[dim + 1 :]), x.dtype)
+    out = lax.dynamic_update_slice_in_dim(out, x, position * rows, axis=dim)
+    from_left = from_right = x
+    halfway = size // 2
+    for step in range(1, halfway + 1):
+        from_left = lax.ppermute(from_left, axis, right)
+        out = lax.dynamic_update_slice_in_dim(
+            out, from_left, (position - step) % size * rows, axis=dim
+        )
+        if step < size - halfway:
+            from_right = lax.ppermute(from_right, axis, behind)
+            out = lax.dynamic_update_slice_in_dim(
+                out, from_right, (position + step) % size * rows, axis=dim
+            )
+    return out
 
 
 def padded_2(value, sides, width):
@@ -129,7 +150,7 @@
     for step_index in reversed(range(STEPS)):
         padded = padded_2(adjoint + forcings[step_index], (("mem", 2), ("lat", 1)), 1)
         adjoint = retreat(padded, wind_margin(1))
-    product = perturbations * lax.all_gather(adjoint, "mem", axis=2, tiled=True)[None]
+    product = perturbations * gather_around(adjoint, "mem", 2)[None]
     projected = jnp.einsum("mlrf,wf->mlrw", product, lon_full, precision=highest)
     columns = lat_full
     banded = lax.psum_scatter(

time: 259 us -> 274 us (1.058)
  blocking collectives: 17.4 us -> 0 us
  waiting for transfers between devices: 136 us -> 149 us
  starting transfers between devices: 58.4 us -> 69 us
  local copies, waits for them, and re-layouts: 11.8 us -> 21.6 us
    all_gather x1 -> x0, blocking collectives: 17.4 us -> none  [body(): lax.all_gather(adjoint, 'mem', axis=2, tiled=True)[None]]
    ppermute x0 -> x7, waiting for transfers between devices: none -> 10.7 us  [the longest x4 8.2 us: gather_around(): from_left = lax.ppermute(from_left, axis, right)]
    ppermute x0 -> x7, starting transfers between devices: none -> 10 us  [the longest x3 6.74 us: gather_around(): from_right = lax.ppermute(from_right, axis, behind)]
    dynamic_update_slice x0 -> x8, local copies, waits for them, and re-layouts: none -> 7.76 us  [the longest x4 3.79 us: gather_around(): lax.dynamic_update_slice_in_dim(out, from_left, (position - step) % size...]
    reduce_scatter x1, waiting for transfers between devices: 24.8 us -> 28.9 us  [body(): lax.psum_scatter(jnp.einsum('rc,mlrw->cmlw', columns, projected, precisio...]
    unnamed x31 -> x25, local copies, waits for them, and re-layouts: 5.89 us -> 5.86 us
  transfers between devices with their start and end apart: 27 -> 34, of which waited for: 19 -> 24; matrix products, arithmetic and copies ran while one was open for 6% -> 9% of each run, Pallas kernels for 0% -> 0%
where the time goes in v1:
time: 274 us; the launch traced here: 273 us
  waiting for transfers between devices  149 us (54%)
  starting transfers between devices  69 us (25%)
  local copies, waits for them, and re-layouts  21.6 us (8%)
  between operations  14.5 us (5%)
  other arithmetic  10.7 us (4%)
  matrix products  7.93 us (3%)
    ppermute x12, starting transfers between devices, padded_2(): before = lax.ppermute(last, axis, up)  43.4 us
    all_gather x1, waiting for transfers between devices, body(): lax.all_gather(widened, 'lat', axis=0, tiled=True)  40.2 us
    ppermute x12, waiting for transfers between devices, padded_2(): after = lax.ppermute(initial, axis, down)  36.6 us
    reduce_scatter x1, waiting for transfers between devices, body(): lax.psum_scatter(jnp.einsum('rc,mlrw->cmlw', columns, projected, precisio...  28.9 us
    unnamed x4, waiting for transfers between devices  23.1 us
    ppermute x12, starting transfers between devices, padded_2(): after = lax.ppermute(initial, axis, down)  15.5 us
    ppermute x12, waiting for transfers between devices, padded_2(): before = lax.ppermute(last, axis, up)  9.47 us
    ppermute x4, waiting for transfers between devices, gather_around(): from_left = lax.ppermute(from_left, axis, right)  8.2 us
  transfers between devices with their start and end apart: 34, of which 24 were waited for; matrix products, arithmetic and copies ran while one was open for 9% of the time, Pallas kernels for 0%

profile of v1, /device:TPU:0, one launch (start us, length us, event | category | flops | bytes accessed | tf_op | source)
XLA Modules:
  0.0 272.7 jit_solution(11452026398968652341)
XLA Ops:
  8.1 1.8 fusion.53
  10.0 1.5 fusion.76
  11.5 3.0 %collective-permute-start.4 = (f32[2,32,4]{2,1,0:T(8,128)}, f32[2,32,4]{2,1,0:T(8,128)}, u32[]{:S(2)}, u32[]{:S(2)}) collective-permute-start(f32[2,32,4]{2,1,0:T(8,128)} %get-tuple-element.62), channel_id=1, source_target_pairs={{0,4},{4,8},{8,12},{12,16},{16,20},{20,24},{24,28},{1,5},{5,9},{9,... | collective-permute-start | bytes 3080 | tf_op jit(solution)/shard_map/ppermute | solution.py:40
  16.2 1.3 multiply_bitcast_fusion.3
  18.3 40.2 %all-gather.2.cloned.1.call-done = f32[32,4,8,512]{3,0,2,1:T(8,128)} async-done(((f32[8,4,8,512]{3,0,2,1:T(8,128)}), f32[32,4,8,512]{3,0,2,1:T(8,128)}) %all-gather.2.cloned.1.call-update) | async-done | bytes 2097168 | tf_op jit(solution)/shard_map/all_gather | solution.py:121
  58.5 3.7 %fusion = f32[8,32,512]{2,1,0:T(8,128)} fusion(bf16[4,8,32,512]{3,2,1,0:T(8,128)(2,1)S(1)} %copy-done.1, f32[32,4,8,512]{3,0,2,1:T(8,128)} %all-gather.2.cloned.1.call-done, bf16[32,32]{1,0:T(8,128)(2,1)} %param.10), kind=kOutput, calls=%fused_computation.2 | convolution fusion | flops 202768384 | bytes 3672064 | tf_op jit(solution)/shard_map/rc,cmlf->mlrf/dot_general | solution.py:118
  62.2 1.8 copy.282
  64.0 1.4 reshape.299
  66.4 2.1 collective-permute-start.6
  71.5 2.4 collective-permute-done.7
  75.5 23.0 %reduce-scatter.7.cloned.1.call-done = f32[64,256]{1,0:T(8,128)} async-done(((f32[512,256]{1,0:T(8,128)}), f32[64,256]{1,0:T(8,128)}) %reduce-scatter.7.cloned.1.call-update) | async-done | bytes 65552
  99.8 1.3 collective-permute-start
  102.5 3.6 %collective-permute-done.1 = f32[8,32,4]{2,1,0:T(8,128)S(1)} collective-permute-done((f32[8,32,4]{2,1,0:T(8,128)S(1)}, f32[8,32,4]{2,1,0:T(8,128)S(1)}, u32[]{:S(2)}, u32[]{:S(2)}) %collective-permute-start.1) | collective-permute-done | bytes 4128 | tf_op jit(solution)/shard_map/ppermute | solution.py:41
  106.3 3.4 %collective-permute-start.2 = (f32[8,4,72]{1,2,0:T(8,128)S(1)}, f32[8,4,72]{1,2,0:T(8,128)S(1)}, u32[]{:S(2)}, u32[]{:S(2)}) collective-permute-start(f32[8,4,72]{1,2,0:T(8,128)S(1)} %copy.254), channel_id=1, source_target_pairs={{0,1},{1,2},{2,3},{4,5},{5,6},{6,7},{8,9},{9,10},{10,11},{12,13},{... | collective-permute-start | bytes 27656 | tf_op jit(solution)/shard_map/ppermute | solution.py:40
  112.0 2.5 collective-permute-done.2
  114.5 4.9 %collective-permute-done.3 = f32[8,4,72]{1,2,0:T(8,128)S(1)} collective-permute-done((f32[8,4,72]{1,2,0:T(8,128)S(1)}, f32[8,4,72]{1,2,0:T(8,128)S(1)}, u32[]{:S(2)}, u32[]{:S(2)}) %collective-permute-start.3) | collective-permute-done | bytes 9248 | tf_op jit(solution)/shard_map/ppermute | solution.py:41
  121.7 4.0 %collective-permute-start.8 = (f32[8,32,1]{1,2,0:T(1,128)S(1)}, f32[8,32,1]{1,2,0:T(1,128)S(1)}, u32[]{:S(2)}, u32[]{:S(2)}) collective-permute-start(f32[8,32,1]{1,2,0:T(1,128)S(1)} %get-tuple-element.40), channel_id=1, source_target_pairs={{0,4},{4,8},{8,12},{12,16},{16,20},{20,24},{24,28},{1,5},{5,9},{9,... | collective-permute-start | bytes 3080 | tf_op jit(solution)/shard_map/ppermute | solution.py:40
  127.0 3.5 %collective-permute-done.9 = f32[8,32,1]{1,2,0:T(1,128)S(1)} collective-permute-done((f32[8,32,1]{1,2,0:T(1,128)S(1)}, f32[8,32,1]{1,2,0:T(1,128)S(1)}, u32[]{:S(2)}, u32[]{:S(2)}) %collective-permute-start.9) | collective-permute-done | bytes 1056 | tf_op jit(solution)/shard_map/ppermute | solution.py:41
  132.0 4.6 %collective-permute-start.11 = (f32[8,1,66]{1,2,0:T(8,128)S(1)}, f32[8,1,66]{1,2,0:T(8,128)S(1)}, u32[]{:S(2)}, u32[]{:S(2)}) collective-permute-start(f32[8,1,66]{1,2,0:T(8,128)S(1)} %get-tuple-element.28), channel_id=1, source_target_pairs={{0,1},{1,2},{2,3},{4,5},{5,6},{6,7},{8,9},{9,10},{10,11},{12,13},{... | collective-permute-start | bytes 6344 | tf_op jit(solution)/shard_map/ppermute | solution.py:40
  136.8 4.3 %collective-permute-done.10 = f32[8,1,66]{1,2,0:T(8,128)S(1)} collective-permute-done((f32[8,1,66]{1,2,0:T(8,128)S(1)}, f32[8,1,66]{1,2,0:T(8,128)S(1)}, u32[]{:S(2)}, u32[]{:S(2)}) %collective-permute-start.10) | collective-permute-done | bytes 2144 | tf_op jit(solution)/shard_map/ppermute | solution.py:41
  141.1 1.7 collective-permute-done.11
  143.6 3.1 %collective-permute-start.12 = (f32[8,32,1]{1,2,0:T(1,128)S(1)}, f32[8,32,1]{1,2,0:T(1,128)S(1)}, u32[]{:S(2)}, u32[]{:S(2)}) collective-permute-start(f32[8,32,1]{1,2,0:T(1,128)S(1)} %get-tuple-element.38), channel_id=1, source_target_pairs={{0,4},{4,8},{8,12},{12,16},{16,20},{20,24},{24,28},{1,5},{5,9},{9,... | collective-permute-start | bytes 3080 | tf_op jit(solution)/shard_map/ppermute | solution.py:40
  148.1 1.8 collective-permute-done.13
  151.3 4.9 %collective-permute-start.15 = (f32[8,1,66]{1,2,0:T(8,128)S(1)}, f32[8,1,66]{1,2,0:T(8,128)S(1)}, u32[]{:S(2)}, u32[]{:S(2)}) collective-permute-start(f32[8,1,66]{1,2,0:T(8,128)S(1)} %get-tuple-element.26), channel_id=1, source_target_pairs={{0,1},{1,2},{2,3},{4,5},{5,6},{6,7},{8,9},{9,10},{10,11},{12,13},{... | collective-permute-start | bytes 6344 | tf_op jit(solution)/shard_map/ppermute | solution.py:40
  156.2 4.1 %collective-permute-done.14 = f32[8,1,66]{1,2,0:T(8,128)S(1)} collective-permute-done((f32[8,1,66]{1,2,0:T(8,128)S(1)}, f32[8,1,66]{1,2,0:T(8,128)S(1)}, u32[]{:S(2)}, u32[]{:S(2)}) %collective-permute-start.14) | collective-permute-done | bytes 2144 | tf_op jit(solution)/shard_map/ppermute | solution.py:41
  160.3 1.7 collective-permute-done.15
  162.9 3.5 %collective-permute-start.16 = (f32[8,32,1]{1,2,0:T(1,128)S(1)}, f32[8,32,1]{1,2,0:T(1,128)S(1)}, u32[]{:S(2)}, u32[]{:S(2)}) collective-permute-start(f32[8,32,1]{1,2,0:T(1,128)S(1)} %get-tuple-element.36), channel_id=1, source_target_pairs={{0,4},{4,8},{8,12},{12,16},{16,20},{20,24},{24,28},{1,5},{5,9},{9,... | collective-permute-start | bytes 3080 | tf_op jit(solution)/shard_map/ppermute | solution.py:40
  167.7 1.8 collective-permute-done.17
  170.9 5.0 %collective-permute-start.19 = (f32[8,1,66]{1,2,0:T(8,128)S(1)}, f32[8,1,66]{1,2,0:T(8,128)S(1)}, u32[]{:S(2)}, u32[]{:S(2)}) collective-permute-start(f32[8,1,66]{1,2,0:T(8,128)S(1)} %get-tuple-element.24), channel_id=1, source_target_pairs={{0,1},{1,2},{2,3},{4,5},{5,6},{6,7},{8,9},{9,10},{10,11},{12,13},{... | collective-permute-start | bytes 6344 | tf_op jit(solution)/shard_map/ppermute | solution.py:40
  175.9 4.2 %collective-permute-done.18 = f32[8,1,66]{1,2,0:T(8,128)S(1)} collective-permute-done((f32[8,1,66]{1,2,0:T(8,128)S(1)}, f32[8,1,66]{1,2,0:T(8,128)S(1)}, u32[]{:S(2)}, u32[]{:S(2)}) %collective-permute-start.18) | collective-permute-done | bytes 2144 | tf_op jit(solution)/shard_map/ppermute | solution.py:41
  180.1 1.7 collective-permute-done.19
  182.6 3.5 %collective-permute-start.20 = (f32[8,32,1]{1,2,0:T(1,128)S(1)}, f32[8,32,1]{1,2,0:T(1,128)S(1)}, u32[]{:S(2)}, u32[]{:S(2)}) collective-permute-start(f32[8,32,1]{1,2,0:T(1,128)S(1)} %get-tuple-element.30), channel_id=1, source_target_pairs={{0,4},{4,8},{8,12},{12,16},{16,20},{20,24},{24,28},{1,5},{5,9},{9,... | collective-permute-start | bytes 3080 | tf_op jit(solution)/shard_map/ppermute | solution.py:40
  187.4 2.0 collective-permute-done.21
  190.9 5.0 %collective-permute-start.23 = (f32[8,1,66]{1,2,0:T(8,128)S(1)}, f32[8,1,66]{1,2,0:T(8,128)S(1)}, u32[]{:S(2)}, u32[]{:S(2)}) collective-permute-start(f32[8,1,66]{1,2,0:T(8,128)S(1)} %get-tuple-element.22), channel_id=1, source_target_pairs={{0,1},{1,2},{2,3},{4,5},{5,6},{6,7},{8,9},{9,10},{10,11},{12,13},{... | collective-permute-start | bytes 6344 | tf_op jit(solution)/shard_map/ppermute | solution.py:40
  195.9 4.2 %collective-permute-done.22 = f32[8,1,66]{1,2,0:T(8,128)S(1)} collective-permute-done((f32[8,1,66]{1,2,0:T(8,128)S(1)}, f32[8,1,66]{1,2,0:T(8,128)S(1)}, u32[]{:S(2)}, u32[]{:S(2)}) %collective-permute-start.22) | collective-permute-done | bytes 2144 | tf_op jit(solution)/shard_map/ppermute | solution.py:41
  200.1 1.7 collective-permute-done.23
  202.6 1.6 collective-permute-start.24
  205.3 4.0 %collective-permute-done.24 = f32[8,32,64]{1,2,0:T(8,128)S(1)} collective-permute-done((f32[8,32,64]{1,2,0:T(8,128)S(1)}, f32[8,32,64]{1,2,0:T(8,128)S(1)}, u32[]{:S(2)}, u32[]{:S(2)}) %collective-permute-start.24) | collective-permute-done | bytes 65568 | tf_op jit(solution)/shard_map/ppermute | solution.py:21
  211.1 2.8 %collective-permute-start.27 = (f32[8,32,64]{1,2,0:T(8,128)S(1)}, f32[8,32,64]{1,2,0:T(8,128)S(1)}, u32[]{:S(2)}, u32[]{:S(2)}) collective-permute-start(f32[8,32,64]{1,2,0:T(8,128)S(1)} %collective-permute-done.25), channel_id=1, source_target_pairs={{0,28},{4,0},{8,4},{12,8},{16,12},{20,16},{24,20},{28,24},{1,29},{... | collective-permute-start | bytes 196616 | tf_op jit(solution)/shard_map/ppermute | solution.py:26
  213.9 2.3 collective-permute-done.26
  217.0 1.7 collective-permute-done.27
  218.7 2.8 %collective-permute-start.29 = (f32[8,32,64]{1,2,0:T(8,128)S(1)}, f32[8,32,64]{1,2,0:T(8,128)}, u32[]{:S(2)}, u32[]{:S(2)}) collective-permute-start(f32[8,32,64]{1,2,0:T(8,128)S(1)} %collective-permute-done.27), channel_id=1, source_target_pairs={{0,28},{4,0},{8,4},{12,8},{16,12},{20,16},{24,20},{28,24},{1,29},{... | collective-permute-start | bytes 196616 | tf_op jit(solution)/shard_map/ppermute | solution.py:26
  221.6 1.8 collective-permute-done.28
  224.1 1.5 dynamic_update_slice.41
  225.7 1.6 dynamic_update_slice.42
  228.5 1.6 dynamic_update_slice.45
  231.1 1.6 dynamic_update_slice.46
  235.7 28.9 %reduce-scatter.5.cloned.1.call-done = f32[8,4,8,128]{3,0,2,1:T(8,128)} async-done(((f32[32,4,8,128]{3,0,2,1:T(8,128)}), f32[8,4,8,128]{3,0,2,1:T(8,128)}) %reduce-scatter.5.cloned.1.call-update) | async-done | bytes 131088 | tf_op jit(solution)/shard_map/reduce_scatter | solution.py:156
  (137 shorter events, 41.8 us)
Async XLA Ops:
  7.2 0.9 copy-start
  7.2 51.3 %copy-start.1 = (bf16[4,8,32,512]{3,2,1,0:T(8,128)(2,1)S(1)}, bf16[4,8,32,512]{3,2,1,0:T(8,128)(2,1)}, u32[]{:S(2)}) copy-start(bf16[4,8,32,512]{3,2,1,0:T(8,128)(2,1)} %param.9) | copy-start | bytes 3145732
  7.2 51.3 %all-gather.2.cloned.1.call-start = ((), (), s32[]{:S(2)}) async-start(), calls=%async_computation.2 | async-start | bytes 2621440 | tf_op jit(solution)/shard_map/all_gather | solution.py:121
  9.9 88.6 %reduce-scatter.7.cloned.1.call-start = ((), (), s32[]{:S(2)}) async-start(), calls=%async_computation.4 | async-start | bytes 589824
  11.5 54.0 %collective-permute-start.4 = (f32[2,32,4]{2,1,0:T(8,128)}, f32[2,32,4]{2,1,0:T(8,128)}, u32[]{:S(2)}, u32[]{:S(2)}) collective-permute-start(f32[2,32,4]{2,1,0:T(8,128)} %get-tuple-element.62), channel_id=1, source_target_pairs={{0,4},{4,8},{8,12},{12,16},{16,20},{20,24},{24,28},{1,5},{5,9},{9,... | collective-permute-start | bytes 3080 | tf_op jit(solution)/shard_map/ppermute | solution.py:40
  14.5 51.0 %collective-permute-start.5 = (f32[2,32,4]{2,1,0:T(8,128)}, f32[2,32,4]{2,1,0:T(8,128)}, u32[]{:S(2)}, u32[]{:S(2)}) collective-permute-start(f32[2,32,4]{2,1,0:T(8,128)} %get-tuple-element.63), channel_id=1, source_target_pairs={{4,0},{8,4},{12,8},{16,12},{20,16},{24,20},{28,24},{5,1},{9,5},{13... | collective-permute-start | bytes 3080 | tf_op jit(solution)/shard_map/ppermute | solution.py:41
  64.0 1.5 copy-start.3
  65.4 199.1 %reduce-scatter.5.cloned.1.call-start = ((), (), s32[]{:S(2)}) async-start(), calls=%async_computation.3 | async-start | bytes 655360 | tf_op jit(solution)/shard_map/reduce_scatter | solution.py:156
  66.4 5.1 %collective-permute-start.6 = (f32[2,4,72]{2,1,0:T(4,128)S(1)}, f32[2,4,72]{2,1,0:T(4,128)S(1)}, u32[]{:S(2)}, u32[]{:S(2)}) collective-permute-start(f32[2,4,72]{2,1,0:T(4,128)S(1)} %get-tuple-element.50), channel_id=1, source_target_pairs={{0,1},{1,2},{2,3},{4,5},{5,6},{6,7},{8,9},{9,10},{10,11},{12,13},{... | collective-permute-start | bytes 6920 | tf_op jit(solution)/shard_map/ppermute | solution.py:40
  68.4 5.5 %collective-permute-start.7 = (f32[2,4,72]{2,1,0:T(4,128)S(1)}, f32[2,4,72]{2,1,0:T(4,128)S(1)}, u32[]{:S(2)}, u32[]{:S(2)}) collective-permute-start(f32[2,4,72]{2,1,0:T(4,128)S(1)} %get-tuple-element.51), channel_id=1, source_target_pairs={{1,0},{2,1},{3,2},{5,4},{6,5},{7,6},{9,8},{10,9},{11,10},{13,12},{... | collective-permute-start | bytes 6920 | tf_op jit(solution)/shard_map/ppermute | solution.py:41
  99.7 20.4 %copy-start.2 = (f32[8,32,64]{2,1,0:T(8,128)}, f32[8,32,64]{2,1,0:T(8,128)S(1)}, u32[]{:S(2)}) copy-start(f32[8,32,64]{2,1,0:T(8,128)S(1)} %broadcast_multiply_fusion.8) | copy-start | bytes 196612
  99.8 2.7 collective-permute-start
  101.1 4.9 %collective-permute-start.1 = (f32[8,32,4]{2,1,0:T(8,128)S(1)}, f32[8,32,4]{2,1,0:T(8,128)S(1)}, u32[]{:S(2)}, u32[]{:S(2)}) collective-permute-start(f32[8,32,4]{2,1,0:T(8,128)S(1)} %get-tuple-element.49), channel_id=1, source_target_pairs={{4,0},{8,4},{12,8},{16,12},{20,16},{24,20},{28,24},{5,1},{9,5},{13... | collective-permute-start | bytes 12296 | tf_op jit(solution)/shard_map/ppermute | solution.py:41
  106.3 8.2 %collective-permute-start.2 = (f32[8,4,72]{1,2,0:T(8,128)S(1)}, f32[8,4,72]{1,2,0:T(8,128)S(1)}, u32[]{:S(2)}, u32[]{:S(2)}) collective-permute-start(f32[8,4,72]{1,2,0:T(8,128)S(1)} %copy.254), channel_id=1, source_target_pairs={{0,1},{1,2},{2,3},{4,5},{5,6},{6,7},{8,9},{9,10},{10,11},{12,13},{... | collective-permute-start | bytes 27656 | tf_op jit(solution)/shard_map/ppermute | solution.py:40
  109.9 9.5 %collective-permute-start.3 = (f32[8,4,72]{1,2,0:T(8,128)S(1)}, f32[8,4,72]{1,2,0:T(8,128)S(1)}, u32[]{:S(2)}, u32[]{:S(2)}) collective-permute-start(f32[8,4,72]{1,2,0:T(8,128)S(1)} %copy.255), channel_id=1, source_target_pairs={{1,0},{2,1},{3,2},{5,4},{6,5},{7,6},{9,8},{10,9},{11,10},{13,12},{... | collective-permute-start | bytes 27656 | tf_op jit(solution)/shard_map/ppermute | solution.py:41
  120.4 1.1 copy-start.5
  120.4 1.1 copy-start.6
  121.1 15.5 %copy-start.8 = (f32[34,66]{1,0:T(8,128)S(1)}, f32[34,66]{1,0:T(8,128)}, u32[]{:S(2)}) copy-start(f32[34,66]{1,0:T(8,128)} %get-tuple-element.52) | copy-start | bytes 26932
  121.1 15.6 %copy-start.7 = (f32[34,66]{1,0:T(8,128)S(1)}, f32[34,66]{1,0:T(8,128)}, u32[]{:S(2)}) copy-start(f32[34,66]{1,0:T(8,128)} %get-tuple-element.53) | copy-start | bytes 26932
  121.7 5.3 %collective-permute-start.8 = (f32[8,32,1]{1,2,0:T(1,128)S(1)}, f32[8,32,1]{1,2,0:T(1,128)S(1)}, u32[]{:S(2)}, u32[]{:S(2)}) collective-permute-start(f32[8,32,1]{1,2,0:T(1,128)S(1)} %get-tuple-element.40), channel_id=1, source_target_pairs={{0,4},{4,8},{8,12},{12,16},{16,20},{20,24},{24,28},{1,5},{5,9},{9,... | collective-permute-start | bytes 3080 | tf_op jit(solution)/shard_map/ppermute | solution.py:40
  125.7 4.8 %collective-permute-start.9 = (f32[8,32,1]{1,2,0:T(1,128)S(1)}, f32[8,32,1]{1,2,0:T(1,128)S(1)}, u32[]{:S(2)}, u32[]{:S(2)}) collective-permute-start(f32[8,32,1]{1,2,0:T(1,128)S(1)} %get-tuple-element.41), channel_id=1, source_target_pairs={{4,0},{8,4},{12,8},{16,12},{20,16},{24,20},{28,24},{5,1},{9,5},{13... | collective-permute-start | bytes 3080 | tf_op jit(solution)/shard_map/ppermute | solution.py:41
  130.7 10.4 %collective-permute-start.10 = (f32[8,1,66]{1,2,0:T(8,128)S(1)}, f32[8,1,66]{1,2,0:T(8,128)S(1)}, u32[]{:S(2)}, u32[]{:S(2)}) collective-permute-start(f32[8,1,66]{1,2,0:T(8,128)S(1)} %get-tuple-element.29), channel_id=1, source_target_pairs={{1,0},{2,1},{3,2},{5,4},{6,5},{7,6},{9,8},{10,9},{11,10},{13,12},{... | collective-permute-start | bytes 6344 | tf_op jit(solution)/shard_map/ppermute | solution.py:41
  132.0 10.8 %collective-permute-start.11 = (f32[8,1,66]{1,2,0:T(8,128)S(1)}, f32[8,1,66]{1,2,0:T(8,128)S(1)}, u32[]{:S(2)}, u32[]{:S(2)}) collective-permute-start(f32[8,1,66]{1,2,0:T(8,128)S(1)} %get-tuple-element.28), channel_id=1, source_target_pairs={{0,1},{1,2},{2,3},{4,5},{5,6},{6,7},{8,9},{9,10},{10,11},{12,13},{... | collective-permute-start | bytes 6344 | tf_op jit(solution)/shard_map/ppermute | solution.py:40
  143.6 4.5 %collective-permute-start.12 = (f32[8,32,1]{1,2,0:T(1,128)S(1)}, f32[8,32,1]{1,2,0:T(1,128)S(1)}, u32[]{:S(2)}, u32[]{:S(2)}) collective-permute-start(f32[8,32,1]{1,2,0:T(1,128)S(1)} %get-tuple-element.38), channel_id=1, source_target_pairs={{0,4},{4,8},{8,12},{12,16},{16,20},{20,24},{24,28},{1,5},{5,9},{9,... | collective-permute-start | bytes 3080 | tf_op jit(solution)/shard_map/ppermute | solution.py:40
  146.8 3.1 %collective-permute-start.13 = (f32[8,32,1]{1,2,0:T(1,128)S(1)}, f32[8,32,1]{1,2,0:T(1,128)S(1)}, u32[]{:S(2)}, u32[]{:S(2)}) collective-permute-start(f32[8,32,1]{1,2,0:T(1,128)S(1)} %get-tuple-element.39), channel_id=1, source_target_pairs={{4,0},{8,4},{12,8},{16,12},{20,16},{24,20},{28,24},{5,1},{9,5},{13... | collective-permute-start | bytes 3080 | tf_op jit(solution)/shard_map/ppermute | solution.py:41
  150.0 10.3 %collective-permute-start.14 = (f32[8,1,66]{1,2,0:T(8,128)S(1)}, f32[8,1,66]{1,2,0:T(8,128)S(1)}, u32[]{:S(2)}, u32[]{:S(2)}) collective-permute-start(f32[8,1,66]{1,2,0:T(8,128)S(1)} %get-tuple-element.27), channel_id=1, source_target_pairs={{1,0},{2,1},{3,2},{5,4},{6,5},{7,6},{9,8},{10,9},{11,10},{13,12},{... | collective-permute-start | bytes 6344 | tf_op jit(solution)/shard_map/ppermute | solution.py:41
  151.3 10.8 %collective-permute-start.15 = (f32[8,1,66]{1,2,0:T(8,128)S(1)}, f32[8,1,66]{1,2,0:T(8,128)S(1)}, u32[]{:S(2)}, u32[]{:S(2)}) collective-permute-start(f32[8,1,66]{1,2,0:T(8,128)S(1)} %get-tuple-element.26), channel_id=1, source_target_pairs={{0,1},{1,2},{2,3},{4,5},{5,6},{6,7},{8,9},{9,10},{10,11},{12,13},{... | collective-permute-start | bytes 6344 | tf_op jit(solution)/shard_map/ppermute | solution.py:40
  162.9 4.8 %collective-permute-start.16 = (f32[8,32,1]{1,2,0:T(1,128)S(1)}, f32[8,32,1]{1,2,0:T(1,128)S(1)}, u32[]{:S(2)}, u32[]{:S(2)}) collective-permute-start(f32[8,32,1]{1,2,0:T(1,128)S(1)} %get-tuple-element.36), channel_id=1, source_target_pairs={{0,4},{4,8},{8,12},{12,16},{16,20},{20,24},{24,28},{1,5},{5,9},{9,... | collective-permute-start | bytes 3080 | tf_op jit(solution)/shard_map/ppermute | solution.py:40
  166.4 3.1 %collective-permute-start.17 = (f32[8,32,1]{1,2,0:T(1,128)S(1)}, f32[8,32,1]{1,2,0:T(1,128)S(1)}, u32[]{:S(2)}, u32[]{:S(2)}) collective-permute-start(f32[8,32,1]{1,2,0:T(1,128)S(1)} %get-tuple-element.37), channel_id=1, source_target_pairs={{4,0},{8,4},{12,8},{16,12},{20,16},{24,20},{28,24},{5,1},{9,5},{13... | collective-permute-start | bytes 3080 | tf_op jit(solution)/shard_map/ppermute | solution.py:41
  169.6 10.4 %collective-permute-start.18 = (f32[8,1,66]{1,2,0:T(8,128)S(1)}, f32[8,1,66]{1,2,0:T(8,128)S(1)}, u32[]{:S(2)}, u32[]{:S(2)}) collective-permute-start(f32[8,1,66]{1,2,0:T(8,128)S(1)} %get-tuple-element.25), channel_id=1, source_target_pairs={{1,0},{2,1},{3,2},{5,4},{6,5},{7,6},{9,8},{10,9},{11,10},{13,12},{... | collective-permute-start | bytes 6344 | tf_op jit(solution)/shard_map/ppermute | solution.py:41
  170.9 10.9 %collective-permute-start.19 = (f32[8,1,66]{1,2,0:T(8,128)S(1)}, f32[8,1,66]{1,2,0:T(8,128)S(1)}, u32[]{:S(2)}, u32[]{:S(2)}) collective-permute-start(f32[8,1,66]{1,2,0:T(8,128)S(1)} %get-tuple-element.24), channel_id=1, source_target_pairs={{0,1},{1,2},{2,3},{4,5},{5,6},{6,7},{8,9},{9,10},{10,11},{12,13},{... | collective-permute-start | bytes 6344 | tf_op jit(solution)/shard_map/ppermute | solution.py:40
  182.6 4.8 %collective-permute-start.20 = (f32[8,32,1]{1,2,0:T(1,128)S(1)}, f32[8,32,1]{1,2,0:T(1,128)S(1)}, u32[]{:S(2)}, u32[]{:S(2)}) collective-permute-start(f32[8,32,1]{1,2,0:T(1,128)S(1)} %get-tuple-element.30), channel_id=1, source_target_pairs={{0,4},{4,8},{8,12},{12,16},{16,20},{20,24},{24,28},{1,5},{5,9},{9,... | collective-permute-start | bytes 3080 | tf_op jit(solution)/shard_map/ppermute | solution.py:40
  186.1 3.3 %collective-permute-start.21 = (f32[8,32,1]{1,2,0:T(1,128)S(1)}, f32[8,32,1]{1,2,0:T(1,128)S(1)}, u32[]{:S(2)}, u32[]{:S(2)}) collective-permute-start(f32[8,32,1]{1,2,0:T(1,128)S(1)} %get-tuple-element.31), channel_id=1, source_target_pairs={{4,0},{8,4},{12,8},{16,12},{20,16},{24,20},{28,24},{5,1},{9,5},{13... | collective-permute-start | bytes 3080 | tf_op jit(solution)/shard_map/ppermute | solution.py:41
  189.6 10.6 %collective-permute-start.22 = (f32[8,1,66]{1,2,0:T(8,128)S(1)}, f32[8,1,66]{1,2,0:T(8,128)S(1)}, u32[]{:S(2)}, u32[]{:S(2)}) collective-permute-start(f32[8,1,66]{1,2,0:T(8,128)S(1)} %get-tuple-element.23), channel_id=1, source_target_pairs={{1,0},{2,1},{3,2},{5,4},{6,5},{7,6},{9,8},{10,9},{11,10},{13,12},{... | collective-permute-start | bytes 6344 | tf_op jit(solution)/shard_map/ppermute | solution.py:41
  190.9 11.0 %collective-permute-start.23 = (f32[8,1,66]{1,2,0:T(8,128)S(1)}, f32[8,1,66]{1,2,0:T(8,128)S(1)}, u32[]{:S(2)}, u32[]{:S(2)}) collective-permute-start(f32[8,1,66]{1,2,0:T(8,128)S(1)} %get-tuple-element.22), channel_id=1, source_target_pairs={{0,1},{1,2},{2,3},{4,5},{5,6},{6,7},{8,9},{9,10},{10,11},{12,13},{... | collective-permute-start | bytes 6344 | tf_op jit(solution)/shard_map/ppermute | solution.py:40
  202.6 6.7 %collective-permute-start.24 = (f32[8,32,64]{1,2,0:T(8,128)S(1)}, f32[8,32,64]{1,2,0:T(8,128)S(1)}, u32[]{:S(2)}, u32[]{:S(2)}) collective-permute-start(f32[8,32,64]{1,2,0:T(8,128)S(1)} %fusion.4), channel_id=1, source_target_pairs={{0,4},{4,8},{8,12},{12,16},{16,20},{20,24},{24,28},{28,0},{1,5},{5... | collective-permute-start | bytes 196616 | tf_op jit(solution)/shard_map/ppermute | solution.py:21
  204.2 6.9 %collective-permute-start.25 = (f32[8,32,64]{1,2,0:T(8,128)S(1)}, f32[8,32,64]{1,2,0:T(8,128)S(1)}, u32[]{:S(2)}, u32[]{:S(2)}) collective-permute-start(f32[8,32,64]{1,2,0:T(8,128)S(1)} %fusion.4), channel_id=1, source_target_pairs={{0,28},{4,0},{8,4},{12,8},{16,12},{20,16},{24,20},{28,24},{1,29},{... | collective-permute-start | bytes 196616 | tf_op jit(solution)/shard_map/ppermute | solution.py:26
  209.4 6.8 %collective-permute-start.26 = (f32[8,32,64]{1,2,0:T(8,128)S(1)}, f32[8,32,64]{1,2,0:T(8,128)S(1)}, u32[]{:S(2)}, u32[]{:S(2)}) collective-permute-start(f32[8,32,64]{1,2,0:T(8,128)S(1)} %collective-permute-done.24), channel_id=1, source_target_pairs={{0,4},{4,8},{8,12},{12,16},{16,20},{20,24},{24,28},{28,0},{1,5},{5... | collective-permute-start | bytes 196616 | tf_op jit(solution)/shard_map/ppermute | solution.py:21
  211.1 7.7 %collective-permute-start.27 = (f32[8,32,64]{1,2,0:T(8,128)S(1)}, f32[8,32,64]{1,2,0:T(8,128)S(1)}, u32[]{:S(2)}, u32[]{:S(2)}) collective-permute-start(f32[8,32,64]{1,2,0:T(8,128)S(1)} %collective-permute-done.25), channel_id=1, source_target_pairs={{0,28},{4,0},{8,4},{12,8},{16,12},{20,16},{24,20},{28,24},{1,29},{... | collective-permute-start | bytes 196616 | tf_op jit(solution)/shard_map/ppermute | solution.py:26
  216.2 7.2 %collective-permute-start.28 = (f32[8,32,64]{1,2,0:T(8,128)S(1)}, f32[8,32,64]{1,2,0:T(8,128)S(1)}, u32[]{:S(2)}, u32[]{:S(2)}) collective-permute-start(f32[8,32,64]{1,2,0:T(8,128)S(1)} %collective-permute-done.26), channel_id=1, source_target_pairs={{0,4},{4,8},{8,12},{12,16},{16,20},{20,24},{24,28},{28,0},{1,5},{5... | collective-permute-start | bytes 196616 | tf_op jit(solution)/shard_map/ppermute | solution.py:21
  218.7 11.3 %collective-permute-start.29 = (f32[8,32,64]{1,2,0:T(8,128)S(1)}, f32[8,32,64]{1,2,0:T(8,128)}, u32[]{:S(2)}, u32[]{:S(2)}) collective-permute-start(f32[8,32,64]{1,2,0:T(8,128)S(1)} %collective-permute-done.27), channel_id=1, source_target_pairs={{0,28},{4,0},{8,4},{12,8},{16,12},{20,16},{24,20},{28,24},{1,29},{... | collective-permute-start | bytes 196616 | tf_op jit(solution)/shard_map/ppermute | solution.py:26
  223.4 9.3 %collective-permute-start.30 = (f32[8,32,64]{1,2,0:T(8,128)S(1)}, f32[8,32,64]{1,2,0:T(8,128)S(1)}, u32[]{:S(2)}, u32[]{:S(2)}) collective-permute-start(f32[8,32,64]{1,2,0:T(8,128)S(1)} %collective-permute-done.28), channel_id=1, source_target_pairs={{0,4},{4,8},{8,12},{12,16},{16,20},{20,24},{24,28},{28,0},{1,5},{5... | collective-permute-start | bytes 196616 | tf_op jit(solution)/shard_map/ppermute | solution.py:21
  228.3 6.1 %copy-start.9 = (bf16[32,32]{1,0:T(8,128)(2,1)S(1)}, bf16[32,32]{1,0:T(8,128)(2,1)}, u32[]{:S(2)}) copy-start(bf16[32,32]{1,0:T(8,128)(2,1)} %param.10) | copy-start | bytes 6148
  232.8 31.7 %copy-start.4 = (bf16[8,4,8,128]{3,2,1,0:T(8,128)(2,1)S(1)}, bf16[8,4,8,128]{3,2,1,0:T(8,128)(2,1)}, u32[]{:S(2)}) copy-start(bf16[8,4,8,128]{3,2,1,0:T(8,128)(2,1)} %param.8) | copy-start | bytes 196612
Sparse Core Ops, SparseCore 0:
  10.1 48.3 all-gather.1
  65.6 32.9 reduce-scatter.6
  235.8 28.6 reduce-scatter.4
